TPU v7x, 32 devices: a whole 2x2x4 slice. The times are simulated.
32 devices in a mesh: tm: 4 (over y, x), tile: 8 (over z, core).
Axes of the slice: x: 2, y: 2, z: 4, core: 2. Of those that a mesh axis runs over, the one named last changes fastest.
Arguments:
- diag_blocks: float32 [16384, 4096], P(('tm', 'tile')), as said below
- coupling: float32 [16384, 4096], P(('tm', 'tile')), as said below
- next_diag: float32 [16384, 4096], P(('tm', 'tile')), as said below
- arrow_now: float32 [128, 4096], P('tm'), may hold values from -0.4375 to 0.4375
- arrow_next: float32 [128, 4096], P('tm'), may hold values from -0.4375 to 0.4375
- arrow_tip: float32 [128, 32], P('tm'), may hold values from -6 to 6
Outputs:
- factor_lower: float32 [16384, 4096], P(('tm', 'tile'))
- coupling_out: float32 [16384, 4096], P(('tm', 'tile'))
- arrow_factor: float32 [128, 4096], P('tm')
- handed_diag: float32 [16384, 4096], P(('tm', 'tile'))
- handed_arrow: float32 [128, 4096], P('tm')
- handed_tip: float32 [128, 32], P('tm')
Inputs may be any that keep to these rules, and one draw needn't show every extreme that they name: `diag_blocks`: each 4096 x 4096 block is symmetric positive definite. `next_diag`: each 4096 x 4096 block is symmetric positive definite. `coupling`: with the diag_blocks block and the next_diag block of its time step, each 4096 x 4096 block forms a symmetric positive definite two-block precision matrix.
All inputs are finite; a program needn't handle non-finite values.
Results may differ from a plain program's by a relative error of at most 0.0001.
Values sent between devices are 32-bit elements; how exact they have to be, the bound alone decides.
No kernel may reach another device: no remote copies, remote signals or barrier semaphores. Data moves between devices by JAX's collectives and lax.ppermute only.
A program may use at most 256 MiB of HBM per device.

v0:
```python
import jax
import jax.numpy as jnp
from jax import lax
from jax.sharding import PartitionSpec as P

precise = lax.Precision.HIGHEST


def broadcast(block, axis, source):
    block = jnp.where(lax.axis_index(axis) == source, block, jnp.zeros_like(block))
    return lax.psum(block, axis)


def shifted(value, axis, steps):
    count = lax.axis_size(axis)
    leading, last = (max(0, -steps), min(count, count - steps))
    return lax.ppermute(value, axis, [(source, source + steps) for source in range(leading, last)])


def outer_rows(left_rows, right_rows):
    return lax.dot_general(
        left_rows,
        right_rows,
        (((1,), (1,)), ((), ())),
        precision=precise,
        preferred_element_type=jnp.float32,
    )


def solve_rows(factor, block):
    return jax.scipy.linalg.solve_triangular(factor, block.T, lower=True).T


def local(diag_blocks, coupling, next_diag, arrow_now, arrow_next, arrow_tip):
    row_count = diag_blocks.shape[0]
    col_count = diag_blocks.shape[1]
    panels = lax.axis_size("tile") // 4
    my_index = lax.axis_index("tile")
    row_ids = my_index * row_count + lax.iota(jnp.int32, row_count)
    work_a, work_c, arrow_a = (diag_blocks, coupling, arrow_now)
    next_d, arrow_b, tip_block = (next_diag, arrow_next, arrow_tip)
    for number in range(panels):
        offset = number * row_count
        factor_offset = number * row_count
        factor_ending = factor_offset + row_count
        pivot_blk = broadcast(work_a[:, factor_offset:factor_ending], "tile", number)
        factor = jnp.linalg.cholesky(pivot_blk)
        factor_local_a = jnp.where(
            (row_ids >= factor_offset)[:, None],
            solve_rows(factor, work_a[:, factor_offset:factor_ending]),
            0.0,
        )
        factor_local_c = solve_rows(factor, work_c[:, factor_offset:factor_ending])
        factor_whole_a = lax.all_gather(factor_local_a, "tile", axis=0, tiled=True)
        factor_whole_c = lax.all_gather(factor_local_c, "tile", axis=0, tiled=True)
        factor_local_r = solve_rows(factor, arrow_a[:, factor_offset:factor_ending])
        panel_k = (
            factor_offset,
            factor_local_a,
            factor_local_c,
            factor_local_r,
            factor_whole_a,
            factor_whole_c,
        )
        store_work_a = work_a
        store_work_c = work_c
        store_arrow_a = arrow_a
        store_offset = panel_k[0]
        store_local_a = panel_k[1]
        store_local_c = panel_k[2]
        store_local_r = panel_k[3]
        ending = store_offset + row_count
        store_work_a = store_work_a.at[:, store_offset:ending].set(store_local_a)
        store_work_c = store_work_c.at[:, store_offset:ending].set(store_local_c)
        store_arrow_a = store_arrow_a.at[:, store_offset:ending].set(store_local_r)
        work_a = store_work_a
        work_c = store_work_c
        arrow_a = store_arrow_a
        col_lo = offset + row_count
        apply_work_a = work_a
        apply_work_c = work_c
        apply_arrow_a = arrow_a
        apply_offset = panel_k[0]
        local_a = panel_k[1]
        apply_local_c = panel_k[2]
        apply_local_r = panel_k[3]
        whole_a = panel_k[4]
        keep_rows = (row_ids >= apply_offset + row_count)[:, None]
        targets = whole_a[col_lo:col_count]
        apply_work_a = apply_work_a.at[:, col_lo:col_count].add(
            -jnp.where(keep_rows, outer_rows(local_a, targets), 0.0)
        )
        apply_work_c = apply_work_c.at[:, col_lo:col_count].add(-outer_rows(apply_local_c, targets))
        apply_arrow_a = apply_arrow_a.at[:, col_lo:col_count].add(
            -outer_rows(apply_local_r, targets)
        )
        work_a = apply_work_a
        work_c = apply_work_c
        arrow_a = apply_arrow_a
        apply_next_d = next_d
        apply_arrow_b = arrow_b
        apply_tip_block = tip_block
        local_c = panel_k[2]
        local_r = panel_k[3]
        whole_c = panel_k[5]
        apply_next_d = apply_next_d - outer_rows(local_c, whole_c)
        apply_arrow_b = apply_arrow_b - outer_rows(local_r, whole_c)
        apply_tip_block = apply_tip_block - outer_rows(local_r, local_r)
        next_d = apply_next_d
        arrow_b = apply_arrow_b
        tip_block = apply_tip_block
    col_ids = lax.iota(jnp.int32, col_count)
    factor_lower = jnp.where(col_ids[None, :] <= row_ids[:, None], work_a, 0.0)
    handed_diag, handed_arrow, handed_tip = shifted((next_d, arrow_b, tip_block), "tm", 1)
    return (factor_lower, work_c, arrow_a, handed_diag, handed_arrow, handed_tip)


def solution(mesh):
    return jax.shard_map(
        local,
        mesh=mesh,
        in_specs=(
            P(("tm", "tile"), None),
            P(("tm", "tile"), None),
            P(("tm", "tile"), None),
            P("tm", None),
            P("tm", None),
            P("tm", None),
        ),
        out_specs=(
            P(("tm", "tile"), None),
            P(("tm", "tile"), None),
            P("tm", None),
            P(("tm", "tile"), None),
            P("tm", None),
            P("tm", None),
        ),
        check_vma=False,
    )
```

profile of v0, /device:TPU:0, one launch (start us, length us, event | category | flops | bytes accessed | tf_op | source)
XLA Modules:
  0.0 914.3 jit_solution(8446192928893483997)
XLA Ops:
  7.2 7.9 copy.105
  15.2 3.4 copy.106
  22.5 61.0 %all-reduce.4.cloned.1.call-done = f32[512,512]{1,0:T(8,128)} async-done(((f32[512,512]{1,0:T(8,128)}), f32[512,512]{1,0:T(8,128)}) %all-reduce.4.cloned.1.call-update) | async-done | bytes 1048592 | tf_op jit(solution)/shard_map/psum | solution.py:11
  86.6 11.7 %cholesky.286 = f32[128,128]{1,0:T(8,128)S(1)} custom-call(f32[128,128]{1,0:T(8,128)S(1)} %copy.14), custom_call_target="Cholesky" | custom-call | tf_op jit(solution)/shard_map/jit(cholesky)/cholesky | solution.py:47
  98.4 9.8 %custom-call.33 = f32[1,128,128]{1,2,0:T(8,128)S(1)} custom-call(f32[1,128,128]{2,1,0:T(8,128)S(1)} %get-tuple-element.246), custom_call_target="InvertDiagBlocksLowerTriangular" | custom-call | tf_op jit(solution)/shard_map/jit(cholesky)/cholesky | solution.py:47
  109.3 11.7 %cholesky.305 = f32[128,128]{1,0:T(8,128)S(1)} custom-call(f32[128,128]{1,0:T(8,128)S(1)} %copy.16), custom_call_target="Cholesky" | custom-call | tf_op jit(solution)/shard_map/jit(cholesky)/cholesky | solution.py:47
  121.1 10.0 %custom-call.34 = f32[1,128,128]{1,2,0:T(8,128)S(1)} custom-call(f32[1,128,128]{2,1,0:T(8,128)S(1)} %get-tuple-element.243), custom_call_target="InvertDiagBlocksLowerTriangular" | custom-call | tf_op jit(solution)/shard_map/jit(cholesky)/cholesky | solution.py:47
  132.0 11.7 %cholesky.326 = f32[128,128]{1,0:T(8,128)S(1)} custom-call(f32[128,128]{1,0:T(8,128)S(1)} %copy.18), custom_call_target="Cholesky" | custom-call | tf_op jit(solution)/shard_map/jit(cholesky)/cholesky | solution.py:47
  144.4 9.8 %custom-call.35 = f32[1,128,128]{1,2,0:T(8,128)S(1)} custom-call(f32[1,128,128]{2,1,0:T(8,128)S(1)} %get-tuple-element.240), custom_call_target="InvertDiagBlocksLowerTriangular" | custom-call | tf_op jit(solution)/shard_map/jit(cholesky)/cholesky | solution.py:47
  155.0 12.2 %cholesky.343 = f32[128,128]{1,0:T(8,128)S(1)} custom-call(f32[128,128]{1,0:T(8,128)S(1)} %copy.20), custom_call_target="Cholesky" | custom-call | tf_op jit(solution)/shard_map/jit(cholesky)/cholesky | solution.py:47
  171.2 7.7 while.24
  178.9 39.3 %custom-call.36 = f32[4,128,128]{1,2,0:T(8,128)S(1)} custom-call(f32[4,128,128]{2,1,0:T(8,128)S(1)} %get-tuple-element.193), custom_call_target="InvertDiagBlocksLowerTriangular" | custom-call | tf_op jit(solution)/shard_map/jit(_solve_triangular)/triangular_solve | solution.py:31
  226.8 3.4 select_dynamic-update-slice_fusion.3
  237.6 73.9 %all-gather.5.cloned.1.call-done = f32[4096,512]{1,0:T(8,128)} async-done(((f32[512,512]{1,0:T(8,128)}), f32[4096,512]{1,0:T(8,128)}) %all-gather.5.cloned.1.call-update) | async-done | bytes 8388624 | tf_op jit(solution)/shard_map/all_gather | solution.py:54
  311.4 17.8 %constant_dynamic-update-slice_fusion.4 = (f32[512,4096]{1,0:T(8,128)}, f32[512,3584]{1,0:T(8,128)S(1)}) fusion(f32[512,4096]{1,0:T(8,128)} %get-tuple-element.217, f32[4096,512]{1,0:T(8,128)} %all-gather.5.cloned.1.call-done, f32[128,512]{0,1:T(8,128)} %copy-done.17, f32[128,512]{0,1:T(8,128)} %copy-done.16, f32[128,512]{0,1:T(8,128)} %copy-done.15, ...), kind=kOutput, calls=%fused_computation.244 | convolution fusion | flops 11280842752 | bytes 30409728 | tf_op jit(solution)/shard_map/dot_general | solution.py:21
  329.3 3.0 copy-done.2
  336.2 2.5 convolution_subtract_fusion.11
  341.1 3.0 select_dynamic-update-slice_fusion.1
  344.0 17.6 %constant_dynamic-update-slice_fusion.3 = (f32[512,4096]{1,0:T(8,128)}, f32[512,3584]{1,0:T(8,128)S(1)}) fusion(f32[512,4096]{1,0:T(8,128)} %select_dynamic-update-slice_fusion.1, f32[4096,512]{1,0:T(8,128)} %all-gather.5.cloned.1.call-done, f32[128,512]{0,1:T(8,128)S(1)} %fusion.130, f32[128,512]{0,1:T(8,128)S(1)} %copy.33, f32[128,512]{0,1:T(8,128)S(1)} %copy.32, ...), kind=kOutput, calls=%fused_computation.243 | convolution fusion | flops 11278745600 | bytes 30408704 | tf_op jit(solution)/shard_map/dot_general | solution.py:21
  361.7 2.9 copy-done.3
  365.6 28.9 %all-reduce.6.cloned.1.call-done = f32[512,512]{0,1:T(8,128)} async-done(((f32[512,512]{0,1:T(8,128)}), f32[512,512]{0,1:T(8,128)}) %all-reduce.6.cloned.1.call-update) | async-done | bytes 1048592 | tf_op jit(solution)/shard_map/psum | solution.py:11
  398.5 11.7 %cholesky.358 = f32[128,128]{1,0:T(8,128)S(1)} custom-call(f32[128,128]{1,0:T(8,128)S(1)} %cholesky.439), custom_call_target="Cholesky" | custom-call | tf_op jit(solution)/shard_map/jit(cholesky)/cholesky | solution.py:47
  410.2 9.8 %custom-call.37 = f32[1,128,128]{1,2,0:T(8,128)S(1)} custom-call(f32[1,128,128]{2,1,0:T(8,128)S(1)} %get-tuple-element.236), custom_call_target="InvertDiagBlocksLowerTriangular" | custom-call | tf_op jit(solution)/shard_map/jit(cholesky)/cholesky | solution.py:47
  423.4 11.7 %cholesky.377 = f32[128,128]{1,0:T(8,128)S(1)} custom-call(f32[128,128]{1,0:T(8,128)S(1)} %cholesky.443), custom_call_target="Cholesky" | custom-call | tf_op jit(solution)/shard_map/jit(cholesky)/cholesky | solution.py:47
  435.1 9.9 %custom-call.38 = f32[1,128,128]{1,2,0:T(8,128)S(1)} custom-call(f32[1,128,128]{2,1,0:T(8,128)S(1)} %get-tuple-element.233), custom_call_target="InvertDiagBlocksLowerTriangular" | custom-call | tf_op jit(solution)/shard_map/jit(cholesky)/cholesky | solution.py:47
  447.5 11.7 %cholesky.398 = f32[128,128]{1,0:T(8,128)S(1)} custom-call(f32[128,128]{1,0:T(8,128)S(1)} %cholesky.448), custom_call_target="Cholesky" | custom-call | tf_op jit(solution)/shard_map/jit(cholesky)/cholesky | solution.py:47
  459.3 9.8 %custom-call.39 = f32[1,128,128]{1,2,0:T(8,128)S(1)} custom-call(f32[1,128,128]{2,1,0:T(8,128)S(1)} %get-tuple-element.230), custom_call_target="InvertDiagBlocksLowerTriangular" | custom-call | tf_op jit(solution)/shard_map/jit(cholesky)/cholesky | solution.py:47
  470.5 11.7 %cholesky.415 = f32[128,128]{1,0:T(8,128)S(1)} custom-call(f32[128,128]{1,0:T(8,128)S(1)} %convolution_subtract_fusion.18), custom_call_target="Cholesky" | custom-call | tf_op jit(solution)/shard_map/jit(cholesky)/cholesky | solution.py:47
  488.9 11.9 %while.25 = (s32[]{:T(128)}, f32[512,512]{1,0:T(8,128)}, s32[4,2]{0,1:T(2,128)S(1)}, f32[4,128,128]{2,1,0:T(8,128)S(1)}, s32[]{:T(128)}) while((s32[]{:T(128)}, f32[512,512]{1,0:T(8,128)}, s32[4,2]{0,1:T(2,128)S(1)}, f32[4,128,128]{2,1,0:T(8,128)S(1)}, s32[]{:T(128)}) %tuple.143), condition=%wide.while_cond.12.clone, body=%wide.while_body.12.clone.sunk | while | flops 2 | bytes 131189 | solution.py:31
  500.8 39.3 %custom-call.40 = f32[4,128,128]{1,2,0:T(8,128)S(1)} custom-call(f32[4,128,128]{2,1,0:T(8,128)S(1)} %get-tuple-element.194), custom_call_target="InvertDiagBlocksLowerTriangular" | custom-call | tf_op jit(solution)/shard_map/jit(_solve_triangular)/triangular_solve | solution.py:31
  548.2 2.6 convolution_subtract_fusion.10
  567.6 2.7 convolution_subtract_fusion.12
  571.5 3.5 select_dynamic-update-slice_fusion.2
  579.8 17.3 %fusion.92 = f32[512,4096]{1,0:T(8,128)} fusion(f32[4096,512]{1,0:T(8,128)} %all-gather.9.cloned.1.call-done, f32[128,512]{0,1:T(8,128)S(1)} %fusion.130, f32[128,512]{0,1:T(8,128)S(1)} %copy.33, f32[128,512]{0,1:T(8,128)S(1)} %copy.32, f32[128,512]{0,1:T(8,128)S(1)} %copy.31), kind=kOutput, calls=%fused_computation.136 | convolution fusion | flops 12885688320 | bytes 17825792 | tf_op jit(solution)/shard_map/dot_general | solution.py:21
  597.0 37.2 %all-gather.11.cloned.1.call-done = f32[4096,512]{1,0:T(8,128)} async-done(((f32[512,512]{1,0:T(8,128)}), f32[4096,512]{1,0:T(8,128)}) %all-gather.11.cloned.1.call-update) | async-done | bytes 8388624 | tf_op jit(solution)/shard_map/all_gather | solution.py:55
  634.2 21.0 %subtract_subtract_fusion = f32[512,4096]{1,0:T(8,128)} fusion(f32[512,4096]{1,0:T(8,128)} %param.37, f32[512,4096]{1,0:T(8,128)} %fusion.92, f32[4096,512]{1,0:T(8,128)} %all-gather.11.cloned.1.call-done, f32[128,512]{0,1:T(8,128)S(1)} %fusion.140, f32[128,512]{0,1:T(8,128)S(1)} %copy.37, f32[128,512]{0,1:T(8,128)S(1)} %copy.36, f32[128,512]{0,1:T(8,128)S(1)} %copy.35), kind=kOutput, calls=%fused_computation.4 | convolution fusion | flops 12889882624 | bytes 34603008 | tf_op jit(solution)/shard_map/dot_general | solution.py:21
  655.2 6.9 collective-permute-start
  664.0 9.2 %fusion.21 = f32[32,3584]{1,0:T(8,128)S(1)} fusion(f32[4096,512]{1,0:T(8,128)} %all-gather.5.cloned.1.call-done, f32[32,4096]{1,0:T(8,128)S(1)} %fusion.115, f32[128,32]{0,1:T(8,128)S(1)} %fusion.129, f32[128,32]{0,1:T(8,128)S(1)} %fusion.126, f32[128,32]{0,1:T(8,128)S(1)} %fusion.123, f32[128,32]{0,1:T(8,128)S(1)} %fusion.122), kind=kOutput, calls=%fused_computation.27 | convolution fusion | flops 704921600 | bytes 8323072 | tf_op jit(solution)/shard_map/dot_general | solution.py:21
  673.4 7.6 convolution_subtract_fusion.1
  687.0 2.9 select_dynamic-update-slice_fusion
  690.5 149.0 %collective-permute-done.2 = f32[32,32]{1,0:T(8,128)S(1)} collective-permute-done((f32[32,32]{1,0:T(8,128)S(1)}, f32[32,32]{1,0:T(8,128)S(1)}, u32[]{:S(2)}, u32[]{:S(2)}) %collective-permute-start.2) | collective-permute-done | bytes 4128 | tf_op jit(solution)/shard_map/ppermute | solution.py:17
  839.6 7.6 convolution_subtract_fusion
  847.2 5.4 collective-permute-start.1
  852.7 15.2 %fusion.7 = f32[512,4096]{1,0:T(8,128)} fusion(f32[512,4096]{1,0:T(8,128)} %get-tuple-element.215, f32[4096,512]{1,0:T(8,128)} %all-gather.7.cloned.1.call-done, pred[512]{0:T(512)(128)(4,1)S(1)} %fusion.166, f32[128,512]{0,1:T(8,128)S(1)} %copy-done.13, f32[128,512]{0,1:T(8,128)S(1)} %copy-done.11, f32[128,512]{0,1:T(8,128)S(1)} %copy-done.10, ...), kind=kOutput, calls=%fused_computation.17 | convolution fusion | flops 9669443584 | bytes 19923968 | tf_op jit(solution)/shard_map/dot_general | solution.py:21
  867.9 8.8 fusion
  876.7 14.0 %fusion.6 = f32[512,4096]{1,0:T(8,128)} fusion(f32[512,4096]{1,0:T(8,128)} %select_dynamic-update-slice_fusion, f32[4096,512]{1,0:T(8,128)S(1)} %copy-done, f32[128,512]{0,1:T(8,128)S(1)} %fusion.140, f32[128,512]{0,1:T(8,128)S(1)} %copy.37, f32[128,512]{0,1:T(8,128)S(1)} %copy.36, f32[128,512]{0,1:T(8,128)S(1)} %copy.35), kind=kOutput, calls=%fused_computation.15 | convolution fusion | flops 9667608576 | bytes 19922944 | tf_op jit(solution)/shard_map/dot_general | solution.py:21
  890.6 5.9 fusion.32
  896.5 8.0 copy.109
  (222 shorter events, 111.3 us)
Async XLA Ops:
  7.2 76.3 %all-reduce.4.cloned.1.call-start = ((), (), s32[]{:S(2)}) async-start(), calls=%async_computation | async-start | bytes 2097152 | tf_op jit(solution)/shard_map/psum | solution.py:11
  7.2 7.9 copy-start.4
  15.1 3.4 copy-start.25
  21.8 289.6 %all-gather.5.cloned.1.call-start = ((), (), s32[]{:S(2)}) async-start(), calls=%async_computation.1 | async-start | bytes 9437184 | tf_op jit(solution)/shard_map/all_gather | solution.py:54
  218.2 6.0 copy-start.18
  218.8 11.5 %copy-start.14 = (f32[128,512]{0,1:T(8,128)}, f32[128,512]{0,1:T(8,128)S(1)}, u32[]{:S(2)}) copy-start(f32[128,512]{0,1:T(8,128)S(1)} %copy.21) | copy-start | bytes 786436
  219.9 10.4 %copy-start.15 = (f32[128,512]{0,1:T(8,128)}, f32[128,512]{0,1:T(8,128)S(1)}, u32[]{:S(2)}) copy-start(f32[128,512]{0,1:T(8,128)S(1)} %copy.22) | copy-start | bytes 786436
  221.4 0.7 copy-start.22
  225.3 5.0 copy-start.16
  225.3 8.4 copy-start.19
  226.8 3.5 copy-start.17
  230.3 164.2 %all-reduce.6.cloned.1.call-start = ((), (), s32[]{:S(2)}) async-start(), calls=%async_computation.2 | async-start | bytes 2097152 | tf_op jit(solution)/shard_map/psum | solution.py:11
  231.7 97.6 %copy-start.7 = (f32[512,512]{0,1:T(8,128)}, f32[512,512]{0,1:T(8,128)S(1)}, u32[]{:S(2)}) copy-start(f32[512,512]{0,1:T(8,128)S(1)} %slice_bitcast_fusion.1) | copy-start | bytes 3145732
  329.3 3.0 copy-start.2
  336.1 243.6 %all-gather.9.cloned.1.call-start = ((), (), s32[]{:S(2)}) async-start(), calls=%async_computation.4 | async-start | bytes 9437184 | tf_op jit(solution)/shard_map/all_gather | solution.py:55
  341.0 293.2 %all-gather.11.cloned.1.call-start = ((), (), s32[]{:S(2)}) async-start(), calls=%async_computation.5 | async-start | bytes 9437184 | tf_op jit(solution)/shard_map/all_gather | solution.py:55
  361.7 2.9 copy-start.3
  397.5 1.0 copy-start.8
  422.7 0.7 copy-start.23
  540.2 5.8 copy-start.20
  553.1 299.6 %all-gather.7.cloned.1.call-start = ((), (), s32[]{:S(2)}) async-start(), calls=%async_computation.3 | async-start | bytes 9437184 | tf_op jit(solution)/shard_map/all_gather | solution.py:54
  571.5 8.3 copy-start.12
  597.0 66.1 %copy-start.26 = (f32[32,32]{1,0:T(8,128)S(1)}, f32[32,32]{1,0:T(8,128)}, u32[]{:S(2)}) copy-start(f32[32,32]{1,0:T(8,128)} %param.40) | copy-start | bytes 12292
  597.0 66.3 %copy-start.5 = (f32[32,4096]{1,0:T(8,128)S(1)}, f32[32,4096]{1,0:T(8,128)}, u32[]{:S(2)}) copy-start(f32[32,4096]{1,0:T(8,128)} %copy.107) | copy-start | bytes 1572868
  655.2 18.1 %copy-start.1 = (f32[4096,512]{1,0:T(8,128)S(1)}, f32[4096,512]{1,0:T(8,128)}, u32[]{:S(2)}) copy-start(f32[4096,512]{1,0:T(8,128)} %all-gather.9.cloned.1.call-done) | copy-start | bytes 25165828
  655.2 18.1 %copy-start.24 = (f32[32,4096]{1,0:T(8,128)S(1)}, f32[32,4096]{1,0:T(8,128)}, u32[]{:S(2)}) copy-start(f32[32,4096]{1,0:T(8,128)} %param.39) | copy-start | bytes 1572868
  655.2 241.3 %collective-permute-start = (f32[512,4096]{1,0:T(8,128)}, f32[512,4096]{1,0:T(8,128)}, u32[]{:S(2)}, u32[]{:S(2)}) collective-permute-start(f32[512,4096]{1,0:T(8,128)} %subtract_subtract_fusion), channel_id=1, source_target_pairs={{0,8},{8,16},{16,24},{1,9},{9,17},{17,25},{2,10},{10,18},{18,26},{... | collective-permute-start | bytes 25165832 | tf_op jit(solution)/shard_map/ppermute | solution.py:17
  664.0 17.0 %copy-start.21 = (f32[4,128,128]{1,2,0:T(8,128)S(1)}, f32[4,128,128]{1,2,0:T(8,128)}, u32[]{:S(2)}) copy-start(f32[4,128,128]{1,2,0:T(8,128)} %copy-done.20) | copy-start | bytes 786436
  664.0 175.5 %slice-start = ((s8[8388608]{0:T(1024)(128)(4,1)}), s8[4194304]{0:T(1024)(128)(4,1)S(1)}, s32[]{:S(2)}) async-start(s8[8388608]{0:T(1024)(128)(4,1)} %bitcast.194), calls=%async_computation.6 | async-start | bytes 8388608
  673.4 166.2 %slice-start.1 = ((s8[8388608]{0:T(1024)(128)(4,1)}), s8[4194304]{0:T(1024)(128)(4,1)S(1)}, s32[]{:S(2)}) async-start(s8[8388608]{0:T(1024)(128)(4,1)} %bitcast.194), calls=%async_computation.7 | async-start | bytes 8388608
  681.0 171.7 %copy-start.9 = (f32[128,512]{0,1:T(8,128)S(1)}, f32[128,512]{0,1:T(8,128)}, u32[]{:S(2)}) copy-start(f32[128,512]{0,1:T(8,128)} %copy.27) | copy-start | bytes 786436
  681.0 171.7 %copy-start.10 = (f32[128,512]{0,1:T(8,128)S(1)}, f32[128,512]{0,1:T(8,128)}, u32[]{:S(2)}) copy-start(f32[128,512]{0,1:T(8,128)} %copy.28) | copy-start | bytes 786436
  681.0 171.7 %copy-start.11 = (f32[128,512]{0,1:T(8,128)S(1)}, f32[128,512]{0,1:T(8,128)}, u32[]{:S(2)}) copy-start(f32[128,512]{0,1:T(8,128)} %copy.29) | copy-start | bytes 786436
  681.0 171.7 %copy-start.13 = (f32[128,512]{0,1:T(8,128)S(1)}, f32[128,512]{0,1:T(8,128)}, u32[]{:S(2)}) copy-start(f32[128,512]{0,1:T(8,128)} %copy-done.12) | copy-start | bytes 786436
  685.5 154.0 %collective-permute-start.2 = (f32[32,32]{1,0:T(8,128)S(1)}, f32[32,32]{1,0:T(8,128)S(1)}, u32[]{:S(2)}, u32[]{:S(2)}) collective-permute-start(f32[32,32]{1,0:T(8,128)S(1)} %convolution_subtract_fusion.20), channel_id=1, source_target_pairs={{0,8},{8,16},{16,24},{1,9},{9,17},{17,25},{2,10},{10,18},{18,26},{... | collective-permute-start | bytes 12296 | tf_op jit(solution)/shard_map/ppermute | solution.py:17
  847.2 49.3 %collective-permute-start.1 = (f32[32,4096]{1,0:T(8,128)S(1)}, f32[32,4096]{1,0:T(8,128)}, u32[]{:S(2)}, u32[]{:S(2)}) collective-permute-start(f32[32,4096]{1,0:T(8,128)S(1)} %convolution_subtract_fusion), channel_id=1, source_target_pairs={{0,8},{8,16},{16,24},{1,9},{9,17},{17,25},{2,10},{10,18},{18,26},{... | collective-permute-start | bytes 1572872 | tf_op jit(solution)/shard_map/ppermute | solution.py:17
  867.9 8.8 copy-start
  896.5 8.0 copy-start.6
Sparse Core Ops, SparseCore 0:
  22.0 61.4 all-reduce.3
  230.4 81.0 all-gather.4
  336.3 58.1 all-reduce.5
  395.9 81.0 all-gather.8
  553.2 80.9 all-gather.10
  635.7 80.5 all-gather.6
where the time goes:
time: 926 us; the launch traced here: 914 us
  waiting for transfers between devices  350 us (38%)
  other arithmetic  271 us (29%)
  matrix products  189 us (20%)
  local copies, waits for them, and re-layouts  68.5 us (7%)
  between operations  20.9 us (2%)
  starting transfers between devices  14.1 us (2%)
    another operation x29, other arithmetic, local(): factor = jnp.linalg.cholesky(pivot_blk)  158 us
    ppermute x3, waiting for transfers between devices, shifted(): lax.ppermute(value, axis, [(source, source + steps) for source in range(l...  149 us
    dot_general x12, matrix products, outer_rows(): lax.dot_general(left_rows, right_rows, (((1,), (1,)), ((), ())), precisio...  134 us
    psum x2, waiting for transfers between devices, broadcast(): return lax.psum(block, axis)  89.8 us
    another operation x5, other arithmetic, solve_rows(): return jax.scipy.linalg.solve_triangular(factor, block.T, lower=True).T  79.9 us
    all_gather x2, waiting for transfers between devices, local(): factor_whole_a = lax.all_gather(factor_local_a, 'tile', axis=0, tiled=True)  73.9 us
    another operation x42, matrix products, solve_rows(): return jax.scipy.linalg.solve_triangular(factor, block.T, lower=True).T  47 us
    all_gather x2, waiting for transfers between devices, local(): factor_whole_c = lax.all_gather(factor_local_c, 'tile', axis=0, tiled=True)  37.2 us
  transfers between devices with their start and end apart: 9, of which 5 were waited for; matrix products, arithmetic and copies ran while one was open for 36% of the time, Pallas kernels for 0%

commit v1 on v0

--- a/solution.py
+++ b/solution.py
@@ -52,7 +52,31 @@
         )
         factor_local_c = solve_rows(factor, work_c[:, factor_offset:factor_ending])
         factor_whole_a = lax.all_gather(factor_local_a, "tile", axis=0, tiled=True)
-        factor_whole_c = lax.all_gather(factor_local_c, "tile", axis=0, tiled=True)
+        devices, place, extent = (
+            lax.axis_size("tile"),
+            lax.axis_index("tile"),
+            factor_local_c.shape[0],
+        )
+        forward = [(i, (i + 1) % devices) for i in range(devices)]
+        behind = [(i, (i - 1) % devices) for i in range(devices)]
+        out = jnp.zeros(
+            (*factor_local_c.shape[:0], devices * extent, *factor_local_c.shape[0 + 1 :]),
+            factor_local_c.dtype,
+        )
+        out = lax.dynamic_update_slice_in_dim(out, factor_local_c, place * extent, axis=0)
+        from_left = from_right = factor_local_c
+        halfway = devices // 2
+        for step in range(1, halfway + 1):
+            from_left = lax.ppermute(from_left, "tile", forward)
+            out = lax.dynamic_update_slice_in_dim(
+                out, from_left, (place - step) % devices * extent, axis=0
+            )
+            if step < devices - halfway:
+                from_right = lax.ppermute(from_right, "tile", behind)
+                out = lax.dynamic_update_slice_in_dim(
+                    out, from_right, (place + step) % devices * extent, axis=0
+                )
+        factor_whole_c = out
         factor_local_r = solve_rows(factor, arrow_a[:, factor_offset:factor_ending])
         panel_k = (
             factor_offset,

time: 926 us -> 1080 us (1.17)
  waiting for transfers between devices: 350 us -> 472 us
  local copies, waits for them, and re-layouts: 68.5 us -> 88.6 us
  starting transfers between devices: 14.1 us -> 30.8 us
    ppermute x0 -> x14, waiting for transfers between devices: none -> 178 us  [the longest x8 171 us: local(): from_left = lax.ppermute(from_left, 'tile', forward)]
    all_gather x2 -> x0, waiting for transfers between devices: 37.2 us -> none  [local(): factor_whole_c = lax.all_gather(factor_local_c, 'tile', axis=0, tiled=True)]
    all_gather x2, waiting for transfers between devices: 73.9 us -> 51 us  [local(): factor_whole_a = lax.all_gather(factor_local_a, 'tile', axis=0, tiled=True)]
    dynamic_update_slice x0 -> x14, local copies, waits for them, and re-layouts: none -> 21.3 us  [the longest x8 11.8 us: local(): lax.dynamic_update_slice_in_dim(out, from_left, (place - step) % devices...]
    ppermute x0 -> x14, starting transfers between devices: none -> 19.7 us  [the longest x6 19.4 us: local(): from_right = lax.ppermute(from_right, 'tile', behind)]
    unnamed x64 -> x66, local copies, waits for them, and re-layouts: 30.9 us -> 30 us
  transfers between devices with their start and end apart: 9 -> 21, of which waited for: 5 -> 13; matrix products, arithmetic and copies ran while one was open for 36% -> 30% of each run, Pallas kernels for 0% -> 0%
where the time goes in v1:
time: 1080 us; the launch traced here: 1070 us
  waiting for transfers between devices  472 us (44%)
  other arithmetic  271 us (25%)
  matrix products  185 us (17%)
  local copies, waits for them, and re-layouts  88.6 us (8%)
  starting transfers between devices  30.8 us (3%)
  between operations  20.6 us (2%)
    ppermute x8, waiting for transfers between devices, local(): from_left = lax.ppermute(from_left, 'tile', forward)  171 us
    another operation x29, other arithmetic, local(): factor = jnp.linalg.cholesky(pivot_blk)  158 us
    ppermute x3, waiting for transfers between devices, shifted(): lax.ppermute(value, axis, [(source, source + steps) for source in range(l...  146 us
    dot_general x12, matrix products, outer_rows(): lax.dot_general(left_rows, right_rows, (((1,), (1,)), ((), ())), precisio...  133 us
    psum x2, waiting for transfers between devices, broadcast(): return lax.psum(block, axis)  97.4 us
    another operation x5, other arithmetic, solve_rows(): return jax.scipy.linalg.solve_triangular(factor, block.T, lower=True).T  79.9 us
    all_gather x2, waiting for transfers between devices, local(): factor_whole_a = lax.all_gather(factor_local_a, 'tile', axis=0, tiled=True)  51 us
    another operation x42, matrix products, solve_rows(): return jax.scipy.linalg.solve_triangular(factor, block.T, lower=True).T  44 us
  transfers between devices with their start and end apart: 21, of which 13 were waited for; matrix products, arithmetic and copies ran while one was open for 30% of the time, Pallas kernels for 0%

profile of v1, /device:TPU:0, one launch (start us, length us, event | category | flops | bytes accessed | tf_op | source)
XLA Modules:
  0.0 1067.5 jit_solution(4053819786562536089)
XLA Ops:
  7.2 7.9 copy.120
  22.5 61.0 %all-reduce.4.cloned.1.call-done = f32[512,512]{1,0:T(8,128)} async-done(((f32[512,512]{1,0:T(8,128)}), f32[512,512]{1,0:T(8,128)}) %all-reduce.4.cloned.1.call-update) | async-done | bytes 1048592 | tf_op jit(solution)/shard_map/psum | solution.py:11
  86.6 11.7 %cholesky.286 = f32[128,128]{1,0:T(8,128)S(1)} custom-call(f32[128,128]{1,0:T(8,128)S(1)} %copy.14), custom_call_target="Cholesky" | custom-call | tf_op jit(solution)/shard_map/jit(cholesky)/cholesky | solution.py:47
  98.4 9.8 custom-call.33
  109.3 11.7 %cholesky.305 = f32[128,128]{1,0:T(8,128)S(1)} custom-call(f32[128,128]{1,0:T(8,128)S(1)} %copy.16), custom_call_target="Cholesky" | custom-call | tf_op jit(solution)/shard_map/jit(cholesky)/cholesky | solution.py:47
  121.1 10.0 custom-call.34
  132.0 11.7 %cholesky.326 = f32[128,128]{1,0:T(8,128)S(1)} custom-call(f32[128,128]{1,0:T(8,128)S(1)} %copy.18), custom_call_target="Cholesky" | custom-call | tf_op jit(solution)/shard_map/jit(cholesky)/cholesky | solution.py:47
  144.4 9.8 custom-call.35
  155.0 12.1 %cholesky.343 = f32[128,128]{1,0:T(8,128)S(1)} custom-call(f32[128,128]{1,0:T(8,128)S(1)} %copy.20), custom_call_target="Cholesky" | custom-call | tf_op jit(solution)/shard_map/jit(cholesky)/cholesky | solution.py:47
  171.2 8.1 while.24
  179.3 39.3 %custom-call.36 = f32[4,128,128]{1,2,0:T(8,128)S(1)} custom-call(f32[4,128,128]{2,1,0:T(8,128)S(1)} %get-tuple-element.193), custom_call_target="InvertDiagBlocksLowerTriangular" | custom-call | tf_op jit(solution)/shard_map/jit(_solve_triangular)/triangular_solve | solution.py:31
  243.0 3.5 collective-permute-start.1
  246.6 4.5 broadcast.360.clone
  254.4 37.9 %collective-permute-done = f32[512,512]{1,0:T(8,128)} collective-permute-done((f32[512,512]{1,0:T(8,128)}, f32[512,512]{1,0:T(8,128)}, u32[]{:S(2)}, u32[]{:S(2)}) %collective-permute-start) | collective-permute-done | bytes 1048608 | tf_op jit(solution)/shard_map/ppermute | solution.py:70
  292.4 51.0 %all-gather.3.cloned.1.call-done = f32[4096,512]{1,0:T(8,128)} async-done(((f32[512,512]{1,0:T(8,128)}), f32[4096,512]{1,0:T(8,128)}) %all-gather.3.cloned.1.call-update) | async-done | bytes 8388624 | tf_op jit(solution)/shard_map/all_gather | solution.py:54
  343.5 17.5 %constant_dynamic-update-slice_fusion.20 = (f32[512,4096]{1,0:T(8,128)}, f32[512,3584]{1,0:T(8,128)S(1)}) fusion(f32[512,4096]{1,0:T(8,128)} %get-tuple-element.217, f32[4096,512]{1,0:T(8,128)} %all-gather.3.cloned.1.call-done, f32[128,512]{0,1:T(8,128)S(1)} %copy-done.20, f32[128,512]{0,1:T(8,128)S(1)} %copy.23, f32[128,512]{0,1:T(8,128)S(1)} %copy-done.16, ...), kind=kOutput, calls=%fused_computation.261 | convolution fusion | flops 11280842752 | bytes 30409728 | tf_op jit(solution)/shard_map/dot_general | solution.py:21
  367.9 17.7 %constant_dynamic-update-slice_fusion.19 = (f32[512,4096]{1,0:T(8,128)}, f32[512,3584]{1,0:T(8,128)S(1)}) fusion(f32[512,4096]{1,0:T(8,128)} %get-tuple-element.230, f32[4096,512]{1,0:T(8,128)} %all-gather.3.cloned.1.call-done, f32[128,512]{0,1:T(8,128)S(1)} %fusion.132, f32[128,512]{0,1:T(8,128)S(1)} %copy.33, f32[128,512]{0,1:T(8,128)S(1)} %copy.32, ...), kind=kOutput, calls=%fused_computation.260 | convolution fusion | flops 11278745600 | bytes 30408704 | tf_op jit(solution)/shard_map/dot_general | solution.py:21
  389.6 36.4 %all-reduce.6.cloned.1.call-done = f32[512,512]{0,1:T(8,128)} async-done(((f32[512,512]{0,1:T(8,128)}), f32[512,512]{0,1:T(8,128)}) %all-reduce.6.cloned.1.call-update) | async-done | bytes 1048592 | tf_op jit(solution)/shard_map/psum | solution.py:11
  430.0 11.7 %cholesky.358 = f32[128,128]{1,0:T(8,128)S(1)} custom-call(f32[128,128]{1,0:T(8,128)S(1)} %cholesky.439), custom_call_target="Cholesky" | custom-call | tf_op jit(solution)/shard_map/jit(cholesky)/cholesky | solution.py:47
  441.9 9.8 custom-call.37
  454.3 11.7 %cholesky.377 = f32[128,128]{1,0:T(8,128)S(1)} custom-call(f32[128,128]{1,0:T(8,128)S(1)} %cholesky.443), custom_call_target="Cholesky" | custom-call | tf_op jit(solution)/shard_map/jit(cholesky)/cholesky | solution.py:47
  467.4 10.0 custom-call.38
  478.9 11.7 %cholesky.398 = f32[128,128]{1,0:T(8,128)S(1)} custom-call(f32[128,128]{1,0:T(8,128)S(1)} %cholesky.448), custom_call_target="Cholesky" | custom-call | tf_op jit(solution)/shard_map/jit(cholesky)/cholesky | solution.py:47
  491.3 9.8 custom-call.39
  502.6 11.7 %cholesky.415 = f32[128,128]{1,0:T(8,128)S(1)} custom-call(f32[128,128]{1,0:T(8,128)S(1)} %convolution_subtract_fusion.17), custom_call_target="Cholesky" | custom-call | tf_op jit(solution)/shard_map/jit(cholesky)/cholesky | solution.py:47
  518.9 12.0 %while.25 = (s32[]{:T(128)}, f32[512,512]{1,0:T(8,128)}, s32[4,2]{0,1:T(2,128)S(1)}, f32[4,128,128]{2,1,0:T(8,128)S(1)}, s32[]{:T(128)}) while((s32[]{:T(128)}, f32[512,512]{1,0:T(8,128)}, s32[4,2]{0,1:T(2,128)S(1)}, f32[4,128,128]{2,1,0:T(8,128)S(1)}, s32[]{:T(128)}) %tuple.141), condition=%wide.while_cond.12.clone, body=%wide.while_body.12.clone.sunk | while | flops 2 | bytes 131181 | solution.py:31
  531.0 39.3 %custom-call.40 = f32[4,128,128]{1,2,0:T(8,128)S(1)} custom-call(f32[4,128,128]{2,1,0:T(8,128)S(1)} %get-tuple-element.194), custom_call_target="InvertDiagBlocksLowerTriangular" | custom-call | tf_op jit(solution)/shard_map/jit(_solve_triangular)/triangular_solve | solution.py:31
  600.0 3.5 collective-permute-start.3
  603.5 4.0 collective-permute-start.8
  607.5 38.9 %collective-permute-done.7 = f32[512,512]{1,0:T(8,128)} collective-permute-done((f32[512,512]{1,0:T(8,128)S(1)}, f32[512,512]{1,0:T(8,128)}, u32[]{:S(2)}, u32[]{:S(2)}) %collective-permute-start.7) | collective-permute-done | bytes 1048608 | tf_op jit(solution)/shard_map/ppermute | solution.py:70
  649.4 3.7 collective-permute-start.5
  653.1 38.2 %collective-permute-done.4 = f32[512,512]{1,0:T(8,128)} collective-permute-done((f32[512,512]{1,0:T(8,128)}, f32[512,512]{1,0:T(8,128)}, u32[]{:S(2)}, u32[]{:S(2)}) %collective-permute-start.4) | collective-permute-done | bytes 1048608 | tf_op jit(solution)/shard_map/ppermute | solution.py:70
  694.2 3.8 collective-permute-start.10
  707.1 29.2 %collective-permute-done.9 = f32[512,512]{1,0:T(8,128)} collective-permute-done((f32[512,512]{1,0:T(8,128)}, f32[512,512]{1,0:T(8,128)}, u32[]{:S(2)}, u32[]{:S(2)}) %collective-permute-start.9) | collective-permute-done | bytes 1048608 | tf_op jit(solution)/shard_map/ppermute | solution.py:70
  741.3 20.8 %collective-permute-done.6 = f32[512,512]{1,0:T(8,128)} collective-permute-done((f32[512,512]{1,0:T(8,128)}, f32[512,512]{1,0:T(8,128)}, u32[]{:S(2)}, u32[]{:S(2)}) %collective-permute-start.6) | collective-permute-done | bytes 1048608 | tf_op jit(solution)/shard_map/ppermute | solution.py:70
  765.2 17.3 %fusion.94 = f32[512,4096]{1,0:T(8,128)} fusion(f32[4096,512]{1,0:T(8,128)} %constant_dynamic-update-slice_fusion.10, f32[128,512]{0,1:T(8,128)S(1)} %fusion.132, f32[128,512]{0,1:T(8,128)S(1)} %copy.33, f32[128,512]{0,1:T(8,128)S(1)} %copy.32, f32[128,512]{0,1:T(8,128)S(1)} %copy.31), kind=kOutput, calls=%fused_computation.137 | convolution fusion | flops 12885688320 | bytes 17825792 | tf_op jit(solution)/shard_map/dot_general | solution.py:21
  792.1 6.4 collective-permute-done.13
  798.7 18.2 %subtract_subtract_fusion = f32[512,4096]{1,0:T(8,128)} fusion(f32[512,4096]{1,0:T(8,128)} %param.37, f32[512,4096]{1,0:T(8,128)} %fusion.94, f32[4096,512]{1,0:T(8,128)S(1)} %constant_dynamic-update-slice_fusion.2, f32[128,512]{0,1:T(8,128)S(1)} %fusion.142, f32[128,512]{0,1:T(8,128)S(1)} %copy.37, f32[128,512]{0,1:T(8,128)S(1)} %copy.36, ...), kind=kOutput, calls=%fused_computation.4 | convolution fusion | flops 12889882624 | bytes 34603008 | tf_op jit(solution)/shard_map/dot_general | solution.py:21
  816.8 7.0 collective-permute-start.14
  826.3 8.9 fusion.22
  839.5 7.7 fusion.191
  847.2 9.9 fusion.18
  861.6 145.7 %collective-permute-done.16 = f32[32,32]{1,0:T(8,128)S(1)} collective-permute-done((f32[32,32]{1,0:T(8,128)S(1)}, f32[32,32]{1,0:T(8,128)S(1)}, u32[]{:S(2)}, u32[]{:S(2)}) %collective-permute-start.16) | collective-permute-done | bytes 4128 | tf_op jit(solution)/shard_map/ppermute | solution.py:17
  1007.4 15.4 %fusion.7 = f32[512,4096]{1,0:T(8,128)} fusion(f32[512,4096]{1,0:T(8,128)} %get-tuple-element.215, f32[4096,512]{1,0:T(8,128)} %all-gather.5.cloned.1.call-done, pred[512]{0:T(512)(128)(4,1)S(1)} %fusion.168, f32[128,512]{0,1:T(8,128)S(1)} %copy-done.14, f32[128,512]{0,1:T(8,128)S(1)} %copy-done.9, f32[128,512]{0,1:T(8,128)S(1)} %copy-done.10, ...), kind=kOutput, calls=%fused_computation.17 | convolution fusion | flops 9669443584 | bytes 19923968 | tf_op jit(solution)/shard_map/dot_general | solution.py:21
  1022.7 8.8 fusion
  1031.5 5.9 fusion.33
  1037.4 14.0 %fusion.6 = f32[512,4096]{1,0:T(8,128)} fusion(f32[512,4096]{1,0:T(8,128)} %get-tuple-element.228, f32[4096,512]{1,0:T(8,128)S(1)} %copy-done, f32[128,512]{0,1:T(8,128)S(1)} %fusion.142, f32[128,512]{0,1:T(8,128)S(1)} %copy.37, f32[128,512]{0,1:T(8,128)S(1)} %copy.36, f32[128,512]{0,1:T(8,128)S(1)} %copy.35), kind=kOutput, calls=%fused_computation.15 | convolution fusion | flops 9667608576 | bytes 19922944 | tf_op jit(solution)/shard_map/dot_general | solution.py:21
  1051.4 7.8 copy.123
  (261 shorter events, 162.6 us)
Async XLA Ops:
  7.2 76.3 %all-reduce.4.cloned.1.call-start = ((), (), s32[]{:S(2)}) async-start(), calls=%async_computation | async-start | bytes 2097152 | tf_op jit(solution)/shard_map/psum | solution.py:11
  7.2 7.9 copy-start.3
  15.1 3.4 copy-start.28
  21.8 321.6 %all-gather.3.cloned.1.call-start = ((), (), s32[]{:S(2)}) async-start(), calls=%async_computation.1 | async-start | bytes 9437184 | tf_op jit(solution)/shard_map/all_gather | solution.py:54
  218.6 5.1 copy-start.21
  223.8 7.7 copy-start.22
  223.9 5.1 copy-start.15
  224.1 4.9 copy-start.17
  225.5 3.5 copy-start.19
  229.0 197.0 %all-reduce.6.cloned.1.call-start = ((), (), s32[]{:S(2)}) async-start(), calls=%async_computation.2 | async-start | bytes 2097152 | tf_op jit(solution)/shard_map/psum | solution.py:11
  237.4 106.0 %copy-start.16 = (f32[128,512]{0,1:T(8,128)S(1)}, f32[128,512]{0,1:T(8,128)}, u32[]{:S(2)}) copy-start(f32[128,512]{0,1:T(8,128)} %copy-done.15) | copy-start | bytes 786436
  237.4 106.0 %copy-start.18 = (f32[128,512]{0,1:T(8,128)S(1)}, f32[128,512]{0,1:T(8,128)}, u32[]{:S(2)}) copy-start(f32[128,512]{0,1:T(8,128)} %copy-done.17) | copy-start | bytes 786436
  237.4 106.0 %copy-start.20 = (f32[128,512]{0,1:T(8,128)S(1)}, f32[128,512]{0,1:T(8,128)}, u32[]{:S(2)}) copy-start(f32[128,512]{0,1:T(8,128)} %copy-done.19) | copy-start | bytes 786436
  242.3 49.9 %collective-permute-start = (f32[512,512]{1,0:T(8,128)}, f32[512,512]{1,0:T(8,128)}, u32[]{:S(2)}, u32[]{:S(2)}) collective-permute-start(f32[512,512]{1,0:T(8,128)} %fusion.95), channel_id=1, source_target_pairs={{0,1},{1,2},{2,3},{3,4},{4,5},{5,6},{6,7},{7,0},{8,9},{9,10},{10,1... | collective-permute-start | bytes 3145736 | tf_op jit(solution)/shard_map/ppermute | solution.py:70
  243.0 356.9 %collective-permute-start.1 = (f32[512,512]{1,0:T(8,128)}, f32[512,512]{1,0:T(8,128)}, u32[]{:S(2)}, u32[]{:S(2)}) collective-permute-start(f32[512,512]{1,0:T(8,128)} %fusion.95), channel_id=1, source_target_pairs={{0,7},{1,0},{2,1},{3,2},{4,3},{5,4},{6,5},{7,6},{8,15},{9,8},{10,9... | collective-permute-start | bytes 3145736 | tf_op jit(solution)/shard_map/ppermute | solution.py:75
  292.2 311.3 %collective-permute-start.2 = (f32[512,512]{1,0:T(8,128)}, f32[512,512]{1,0:T(8,128)}, u32[]{:S(2)}, u32[]{:S(2)}) collective-permute-start(f32[512,512]{1,0:T(8,128)} %collective-permute-done), channel_id=1, source_target_pairs={{0,1},{1,2},{2,3},{3,4},{4,5},{5,6},{6,7},{7,0},{8,9},{9,10},{10,1... | collective-permute-start | bytes 3145736 | tf_op jit(solution)/shard_map/ppermute | solution.py:70
  361.0 3.0 copy-start.1
  367.6 639.7 %all-gather.5.cloned.1.call-start = ((), (), s32[]{:S(2)}) async-start(), calls=%async_computation.3 | async-start | bytes 9437184 | tf_op jit(solution)/shard_map/all_gather | solution.py:54
  385.6 2.9 copy-start.2
  570.3 11.7 %copy-start.24 = (f32[4,128,128]{1,2,0:T(8,128)}, f32[4,128,128]{1,2,0:T(8,128)S(1)}, u32[]{:S(2)}) copy-start(f32[4,128,128]{1,2,0:T(8,128)S(1)} %custom-call.40) | copy-start | bytes 786436
  579.6 13.2 %copy-start.8 = (f32[128,512]{0,1:T(8,128)}, f32[128,512]{0,1:T(8,128)S(1)}, u32[]{:S(2)}) copy-start(f32[128,512]{0,1:T(8,128)S(1)} %copy.29) | copy-start | bytes 786436
  580.6 11.9 %copy-start.11 = (f32[128,512]{0,1:T(8,128)}, f32[128,512]{0,1:T(8,128)S(1)}, u32[]{:S(2)}) copy-start(f32[128,512]{0,1:T(8,128)S(1)} %copy.27) | copy-start | bytes 786436
  586.3 3.5 copy-start.13
  599.9 46.4 %collective-permute-start.7 = (f32[512,512]{1,0:T(8,128)S(1)}, f32[512,512]{1,0:T(8,128)}, u32[]{:S(2)}, u32[]{:S(2)}) collective-permute-start(f32[512,512]{1,0:T(8,128)S(1)} %fusion.93), channel_id=1, source_target_pairs={{0,1},{1,2},{2,3},{3,4},{4,5},{5,6},{6,7},{7,0},{8,9},{9,10},{10,1... | collective-permute-start | bytes 3145736 | tf_op jit(solution)/shard_map/ppermute | solution.py:70
  600.0 49.4 %collective-permute-start.3 = (f32[512,512]{1,0:T(8,128)}, f32[512,512]{1,0:T(8,128)}, u32[]{:S(2)}, u32[]{:S(2)}) collective-permute-start(f32[512,512]{1,0:T(8,128)} %collective-permute-done.1), channel_id=1, source_target_pairs={{0,7},{1,0},{2,1},{3,2},{4,3},{5,4},{6,5},{7,6},{8,15},{9,8},{10,9... | collective-permute-start | bytes 3145736 | tf_op jit(solution)/shard_map/ppermute | solution.py:75
  603.5 87.8 %collective-permute-start.4 = (f32[512,512]{1,0:T(8,128)}, f32[512,512]{1,0:T(8,128)}, u32[]{:S(2)}, u32[]{:S(2)}) collective-permute-start(f32[512,512]{1,0:T(8,128)} %collective-permute-done.2), channel_id=1, source_target_pairs={{0,1},{1,2},{2,3},{3,4},{4,5},{5,6},{6,7},{7,0},{8,9},{9,10},{10,1... | collective-permute-start | bytes 3145736 | tf_op jit(solution)/shard_map/ppermute | solution.py:70
  603.5 90.7 %collective-permute-start.8 = (f32[512,512]{1,0:T(8,128)S(1)}, f32[512,512]{1,0:T(8,128)}, u32[]{:S(2)}, u32[]{:S(2)}) collective-permute-start(f32[512,512]{1,0:T(8,128)S(1)} %fusion.93), channel_id=1, source_target_pairs={{0,7},{1,0},{2,1},{3,2},{4,3},{5,4},{6,5},{7,6},{8,15},{9,8},{10,9... | collective-permute-start | bytes 3145736 | tf_op jit(solution)/shard_map/ppermute | solution.py:75
  646.3 89.9 %collective-permute-start.9 = (f32[512,512]{1,0:T(8,128)}, f32[512,512]{1,0:T(8,128)}, u32[]{:S(2)}, u32[]{:S(2)}) collective-permute-start(f32[512,512]{1,0:T(8,128)} %collective-permute-done.7), channel_id=1, source_target_pairs={{0,1},{1,2},{2,3},{3,4},{4,5},{5,6},{6,7},{7,0},{8,9},{9,10},{10,1... | collective-permute-start | bytes 3145736 | tf_op jit(solution)/shard_map/ppermute | solution.py:70
  649.4 89.7 %collective-permute-start.5 = (f32[512,512]{1,0:T(8,128)}, f32[512,512]{1,0:T(8,128)}, u32[]{:S(2)}, u32[]{:S(2)}) collective-permute-start(f32[512,512]{1,0:T(8,128)} %collective-permute-done.3), channel_id=1, source_target_pairs={{0,7},{1,0},{2,1},{3,2},{4,3},{5,4},{6,5},{7,6},{8,15},{9,8},{10,9... | collective-permute-start | bytes 3145736 | tf_op jit(solution)/shard_map/ppermute | solution.py:75
  691.3 70.8 %collective-permute-start.6 = (f32[512,512]{1,0:T(8,128)}, f32[512,512]{1,0:T(8,128)}, u32[]{:S(2)}, u32[]{:S(2)}) collective-permute-start(f32[512,512]{1,0:T(8,128)} %collective-permute-done.4), channel_id=1, source_target_pairs={{0,1},{1,2},{2,3},{3,4},{4,5},{5,6},{6,7},{7,0},{8,9},{9,10},{10,1... | collective-permute-start | bytes 3145736 | tf_op jit(solution)/shard_map/ppermute | solution.py:70
  694.2 70.2 %collective-permute-start.10 = (f32[512,512]{1,0:T(8,128)}, f32[512,512]{1,0:T(8,128)}, u32[]{:S(2)}, u32[]{:S(2)}) collective-permute-start(f32[512,512]{1,0:T(8,128)} %collective-permute-done.8), channel_id=1, source_target_pairs={{0,7},{1,0},{2,1},{3,2},{4,3},{5,4},{6,5},{7,6},{8,15},{9,8},{10,9... | collective-permute-start | bytes 3145736 | tf_op jit(solution)/shard_map/ppermute | solution.py:75
  736.2 46.3 %collective-permute-start.11 = (f32[512,512]{1,0:T(8,128)}, f32[512,512]{1,0:T(8,128)S(1)}, u32[]{:S(2)}, u32[]{:S(2)}) collective-permute-start(f32[512,512]{1,0:T(8,128)} %collective-permute-done.9), channel_id=1, source_target_pairs={{0,1},{1,2},{2,3},{3,4},{4,5},{5,6},{6,7},{7,0},{8,9},{9,10},{10,1... | collective-permute-start | bytes 3145736 | tf_op jit(solution)/shard_map/ppermute | solution.py:70
  764.4 27.6 %collective-permute-start.12 = (f32[512,512]{1,0:T(8,128)}, f32[512,512]{1,0:T(8,128)S(1)}, u32[]{:S(2)}, u32[]{:S(2)}) collective-permute-start(f32[512,512]{1,0:T(8,128)} %collective-permute-done.10), channel_id=1, source_target_pairs={{0,7},{1,0},{2,1},{3,2},{4,3},{5,4},{6,5},{7,6},{8,15},{9,8},{10,9... | collective-permute-start | bytes 3145736 | tf_op jit(solution)/shard_map/ppermute | solution.py:75
  782.5 16.0 %collective-permute-start.13 = (f32[512,512]{1,0:T(8,128)S(1)}, f32[512,512]{1,0:T(8,128)S(1)}, u32[]{:S(2)}, u32[]{:S(2)}) collective-permute-start(f32[512,512]{1,0:T(8,128)S(1)} %collective-permute-done.11), channel_id=1, source_target_pairs={{0,1},{1,2},{2,3},{3,4},{4,5},{5,6},{6,7},{7,0},{8,9},{9,10},{10,1... | collective-permute-start | bytes 3145736 | tf_op jit(solution)/shard_map/ppermute | solution.py:70
  798.6 25.3 %copy-start.4 = (f32[32,4096]{1,0:T(8,128)S(1)}, f32[32,4096]{1,0:T(8,128)}, u32[]{:S(2)}) copy-start(f32[32,4096]{1,0:T(8,128)} %copy.122) | copy-start | bytes 1572868
  798.6 25.3 %copy-start.23 = (f32[4,128,128]{1,2,0:T(8,128)S(1)}, f32[4,128,128]{1,2,0:T(8,128)}, u32[]{:S(2)}) copy-start(f32[4,128,128]{1,2,0:T(8,128)} %copy-done.21) | copy-start | bytes 786436
  798.6 26.8 %copy-start.29 = (f32[32,32]{1,0:T(8,128)S(1)}, f32[32,32]{1,0:T(8,128)}, u32[]{:S(2)}) copy-start(f32[32,32]{1,0:T(8,128)} %param.40) | copy-start | bytes 12292
  816.8 18.4 %copy-start.25 = (f32[4,128,128]{1,2,0:T(8,128)S(1)}, f32[4,128,128]{1,2,0:T(8,128)}, u32[]{:S(2)}) copy-start(f32[4,128,128]{1,2,0:T(8,128)} %copy-done.24) | copy-start | bytes 786436
  816.8 190.5 %collective-permute-start.14 = (f32[512,4096]{1,0:T(8,128)}, f32[512,4096]{1,0:T(8,128)}, u32[]{:S(2)}, u32[]{:S(2)}) collective-permute-start(f32[512,4096]{1,0:T(8,128)} %subtract_subtract_fusion), channel_id=1, source_target_pairs={{0,8},{8,16},{16,24},{1,9},{9,17},{17,25},{2,10},{10,18},{18,26},{... | collective-permute-start | bytes 25165832 | tf_op jit(solution)/shard_map/ppermute | solution.py:17
  826.3 20.9 %copy-start.27 = (f32[32,4096]{1,0:T(8,128)S(1)}, f32[32,4096]{1,0:T(8,128)}, u32[]{:S(2)}) copy-start(f32[32,4096]{1,0:T(8,128)} %param.39) | copy-start | bytes 1572868
  839.4 167.9 %copy-start.9 = (f32[128,512]{0,1:T(8,128)S(1)}, f32[128,512]{0,1:T(8,128)}, u32[]{:S(2)}) copy-start(f32[128,512]{0,1:T(8,128)} %copy-done.8) | copy-start | bytes 786436
  839.5 167.9 %copy-start.10 = (f32[128,512]{0,1:T(8,128)S(1)}, f32[128,512]{0,1:T(8,128)}, u32[]{:S(2)}) copy-start(f32[128,512]{0,1:T(8,128)} %copy.28) | copy-start | bytes 786436
  839.5 167.9 %copy-start.12 = (f32[128,512]{0,1:T(8,128)S(1)}, f32[128,512]{0,1:T(8,128)}, u32[]{:S(2)}) copy-start(f32[128,512]{0,1:T(8,128)} %copy-done.11) | copy-start | bytes 786436
  839.5 167.9 %copy-start.14 = (f32[128,512]{0,1:T(8,128)S(1)}, f32[128,512]{0,1:T(8,128)}, u32[]{:S(2)}) copy-start(f32[128,512]{0,1:T(8,128)} %copy-done.13) | copy-start | bytes 786436
  857.2 150.1 %collective-permute-start.15 = (f32[32,4096]{1,0:T(8,128)S(1)}, f32[32,4096]{1,0:T(8,128)S(1)}, u32[]{:S(2)}, u32[]{:S(2)}) collective-permute-start(f32[32,4096]{1,0:T(8,128)S(1)} %fusion.18), channel_id=1, source_target_pairs={{0,8},{8,16},{16,24},{1,9},{9,17},{17,25},{2,10},{10,18},{18,26},{... | collective-permute-start | bytes 1572872 | tf_op jit(solution)/shard_map/ppermute | solution.py:17
  858.8 148.6 %collective-permute-start.16 = (f32[32,32]{1,0:T(8,128)S(1)}, f32[32,32]{1,0:T(8,128)S(1)}, u32[]{:S(2)}, u32[]{:S(2)}) collective-permute-start(f32[32,32]{1,0:T(8,128)S(1)} %convolution_subtract_fusion.19), channel_id=1, source_target_pairs={{0,8},{8,16},{16,24},{1,9},{9,17},{17,25},{2,10},{10,18},{18,26},{... | collective-permute-start | bytes 12296 | tf_op jit(solution)/shard_map/ppermute | solution.py:17
  1022.7 8.8 copy-start
  1037.4 14.0 %copy-start.5 = (f32[32,4096]{1,0:T(8,128)}, f32[32,4096]{1,0:T(8,128)S(1)}, u32[]{:S(2)}) copy-start(f32[32,4096]{1,0:T(8,128)S(1)} %fusion.33) | copy-start | bytes 1572868
  (3 other events, 2.7 us)
Sparse Core Ops, SparseCore 0:
  22.0 61.4 all-reduce.3
  229.1 114.3 all-gather.2
  367.7 58.2 all-reduce.5
  596.1 142.6 all-gather.4
